TPU v7x, 512 devices: a whole 4x4x16 slice. The times are simulated.
512 devices in a mesh: grp: 32 (over y, x, core), sub: 16 (over z).
Axes of the slice: x: 4, y: 4, z: 16, core: 2. Of those that a mesh axis runs over, the one named last changes fastest.
Arguments:
- loads: bfloat16 [32, 16, 16, 1536], P('grp', 'sub'), may hold values from -6 to 6
- boundary_values: float32 [16, 6144], replicated, may hold values from -6 to 6
- dirichlet_ids: int32 [32, 16, 3, 128], P('grp', 'sub'), may hold values from 0 to 6143
- dirichlet_coupling: bfloat16 [32, 16, 3, 512, 128], P('grp', 'sub'), may hold values from -0.5 to 0.5
- local_inverse: bfloat16 [32, 16, 3, 512, 512], P('grp', 'sub'), as said below
- local_schur: bfloat16 [32, 16, 3, 512, 512], P('grp', 'sub')
- corner_coupling: bfloat16 [32, 16, 3, 24, 512], P('grp', 'sub'), may hold values from -0.25 to 0.25
- corner_ids: int32 [32, 16, 3, 24], P('grp', 'sub'), may hold values from 0 to 12287
- coarse_inverse: bfloat16 [12288, 12288], P(('grp', 'sub')), as said below
- row_counts: int32 [32, 16, 18], P('grp', 'sub'), may hold values from 0 to 256, as said below
- slot_of: int32 [32, 16, 1536], P('grp', 'sub'), may hold values from 0 to 1535, each once within a row
Outputs:
- multipliers: float32 [32, 16, 16, 1536], P('grp', 'sub')
- residual: float32 [32, 16, 16, 1536], P('grp', 'sub')
Inputs may be any that keep to these rules, and one draw needn't show every extreme that they name: row_counts[g, s, p] for p < 16 equals row_counts[g, p, s], is 0 for p = s and lies in 1 to 64 otherwise; every device reaches 64 with some peer. Column 16 of device (g, s) equals column 17 of device (g - 1, s), lies in 1 to 256, reaches 256 on some device of every slab boundary, and is 0 in the first slab; column 17 is 0 in the last slab. coarse_inverse is symmetric and positive definite. local_inverse and local_schur are symmetric and positive definite.
All inputs are finite; a program needn't handle non-finite values.
Results may differ from a plain program's by a relative error of at most 0.012.
Values may be sent and summed in bfloat16 or wider, within the bound.
No kernel may reach another device: no remote copies, remote signals or barrier semaphores. Data moves between devices by JAX's collectives and lax.ppermute only.
A program may use at most 64 MiB of HBM per device.

v0:
```python
import jax
import jax.numpy as jnp
from jax import lax
from jax.sharding import PartitionSpec as P

IFACE = 512
SUBS_DEV = 3
LOADS = 16
CORNERS = 24
SLAB_ROWS = 256
ITERS = 2


def extended(cells, sides, width):
    for axis, dim in sides:
        count = lax.axis_size(axis)
        ends = count - 1
        head = lax.slice_in_dim(cells, 0, width, axis=dim)
        tail = lax.slice_in_dim(cells, cells.shape[dim] - width, cells.shape[dim], axis=dim)
        cells = jnp.concatenate(
            [
                lax.ppermute(tail, axis, [(i, (i + 1) % count) for i in range(ends)]),
                cells,
                lax.ppermute(head, axis, [((i + 1) % count, i) for i in range(ends)]),
            ],
            axis=dim,
        )
    return cells


def per_device(
    loads,
    boundary_values,
    dirichlet_ids,
    dirichlet_coupling,
    local_inverse,
    local_schur,
    corner_coupling,
    corner_ids,
    coarse_inverse,
    row_counts,
    slot_of,
):
    load_cases = loads[0, 0]
    fixed_ids = dirichlet_ids[0, 0]
    fixed_coupling = dirichlet_coupling[0, 0]
    inverse_blocks = local_inverse[0, 0]
    schur_blocks = local_schur[0, 0]
    coupling = corner_coupling[0, 0]
    corner_index = corner_ids[0, 0].reshape(-1)
    counts = row_counts[0, 0]
    slots = slot_of[0, 0]
    n_sub = lax.axis_size("sub")
    length = slots.shape[0]
    peer_rows = (length - 2 * SLAB_ROWS) // n_sub
    within = n_sub * peer_rows
    coarse_size = coarse_inverse.shape[1]
    positions = jnp.arange(length, dtype=jnp.int32)
    slot_inverse = jnp.zeros(length, jnp.int32).at[slots].set(positions)
    column = jnp.where(
        positions < within, positions // peer_rows, n_sub + (positions - within) // SLAB_ROWS
    )
    offset = jnp.where(positions < within, positions % peer_rows, (positions - within) % SLAB_ROWS)
    canon_live = (offset < counts[column]).astype(jnp.float32)
    live_mask = canon_live[slot_inverse][None, :]
    peer_index = slots[:within].reshape(n_sub, peer_rows)
    slab_index = slots[within:].reshape(2, SLAB_ROWS)

    def partner(values):
        outgoing = jnp.take(values, peer_index, axis=1)
        incoming = lax.all_to_all(outgoing, "sub", split_axis=1, concat_axis=1, tiled=True).reshape(
            LOADS, within
        )
        slab_part = jnp.take(values, slab_index, axis=1)
        padded = extended(slab_part, (("grp", 1),), 1)
        joined = jnp.concatenate([incoming, padded[:, 0], padded[:, 3]], axis=1)
        return jnp.take(joined, slot_inverse, axis=1)

    def apply_tilde(field_b):
        blocks = field_b.reshape(LOADS, SUBS_DEV, IFACE)
        local_part = jnp.einsum(
            "anm,ram->ran", inverse_blocks, blocks, preferred_element_type=jnp.float32
        )
        corner_terms = jnp.einsum(
            "acm,ram->rac", coupling, blocks, preferred_element_type=jnp.float32
        )
        partial_load = (
            jnp.zeros((LOADS, coarse_size), jnp.float32)
            .at[:, corner_index]
            .add(corner_terms.reshape(LOADS, -1))
        )
        coarse_load = lax.psum(partial_load, ("grp", "sub"))
        owned_values = jnp.einsum(
            "rj,ij->ri",
            coarse_load.astype(jnp.bfloat16),
            coarse_inverse,
            preferred_element_type=jnp.float32,
        )
        coarse_values = lax.all_gather(owned_values, ("grp", "sub"), axis=1, tiled=True)
        at_corners = (
            jnp.take(coarse_values, corner_index, axis=1)
            .astype(jnp.bfloat16)
            .reshape(LOADS, SUBS_DEV, CORNERS)
        )
        correction = jnp.einsum(
            "acm,rac->ram", coupling, at_corners, preferred_element_type=jnp.float32
        )
        return (local_part + correction).reshape(LOADS, length)

    def jumps(values):
        return live_mask * (values - partner(values))

    picked = jnp.take(boundary_values, fixed_ids, axis=1).astype(jnp.bfloat16)
    lifted_part = jnp.einsum(
        "and,rad->ran", fixed_coupling, picked, preferred_element_type=jnp.float32
    ).reshape(LOADS, length)
    lifted = live_mask * (load_cases.astype(jnp.float32) - lifted_part)
    jump_field = jumps(apply_tilde(lifted.astype(jnp.bfloat16)))
    multipliers = jnp.zeros_like(jump_field)
    residual = jump_field
    search = jump_field
    inner_before = jnp.ones((LOADS,), jnp.float32)
    for step in range(ITERS):
        smoothed = jnp.einsum(
            "anm,ram->ran",
            schur_blocks,
            residual.astype(jnp.bfloat16).reshape(LOADS, SUBS_DEV, IFACE),
            preferred_element_type=jnp.float32,
        ).reshape(LOADS, length)
        precond = 0.25 * live_mask * (smoothed - partner(smoothed))
        inner_now = lax.psum(jnp.sum(residual * precond, axis=1), ("grp", "sub"))
        if step == 0:
            search = precond
        else:
            search = precond + (inner_now / inner_before)[:, None] * search
        tilde = apply_tilde(search.astype(jnp.bfloat16))
        image = jumps(tilde)
        curvature = lax.psum(jnp.sum(search * image, axis=1), ("grp", "sub"))
        step_size = (inner_now / curvature)[:, None]
        multipliers = multipliers + step_size * search
        residual = residual - step_size * image
        inner_before = inner_now
    return (multipliers[None, None], residual[None, None])


def solution(mesh):
    in_specs = (
        P("grp", "sub", None, None),
        P(),
        P("grp", "sub", None, None),
        P("grp", "sub", None, None, None),
        P("grp", "sub", None, None, None),
        P("grp", "sub", None, None, None),
        P("grp", "sub", None, None, None),
        P("grp", "sub", None, None),
        P(("grp", "sub"), None),
        P("grp", "sub", None),
        P("grp", "sub", None),
    )
    out_specs = (P("grp", "sub", None, None), P("grp", "sub", None, None))
    return jax.shard_map(
        per_device, mesh=mesh, in_specs=in_specs, out_specs=out_specs, check_vma=False
    )
```

profile of v0, /device:TPU:1, one launch (start us, length us, event | category | flops | bytes accessed | tf_op | source)
XLA Modules:
  0.0 1553.7 jit_solution(18050115892917891328)
XLA Ops:
  7.5 6.2 scatter_custom_fusion
  13.8 2.0 fusion.121
  15.8 4.4 fusion.102
  20.2 6.9 fusion.100
  27.2 8.4 gather_fusion
  35.7 1.7 copy.263
  40.5 4.0 scatter_custom_fusion.1
  44.5 195.8 %all-reduce.4 = bf16[16,12288]{0,1:T(8,128)(2,1)} all-reduce(f32[16,12288]{0,1:T(8,128)} %scatter_custom_fusion.1), channel_id=1, replica_groups=mesh['grp'=32,'sub'=16] {'grp','sub'}, use_global_device_ids=true, to_apply=%region_2.3 | all-reduce | flops 196608 | bytes 1179648 | tf_op jit(solution)/shard_map/psum | solution.py:92
  240.3 2.8 fusion.49
  243.1 120.0 %all-gather = bf16[512,24,16]{1,2,0:T(8,128)(2,1)} all-gather(bf16[1,24,16]{1,2,0:T(8,128)(2,1)S(1)} %fusion.49), channel_id=1, replica_groups=mesh['grp'=32,'sub'=16] {'grp','sub'}, dimensions={0}, use_global_device_ids=true | all-gather | bytes 393984 | tf_op jit(solution)/shard_map/all_gather | solution.py:99
  363.1 4.5 copy.330
  367.6 3.0 gather_fusion.2
  372.6 4.0 gather_fusion.3
  378.6 1.7 reshape.762
  380.3 6.2 all-to-all-start
  387.3 2.8 gather_fusion.4
  391.8 8.2 collective-permute-start
  400.0 3.3 collective-permute-start.1
  411.1 4.8 gather_fusion.5
  419.6 2.8 gather_fusion.7
  422.4 5.1 gather_fusion.6
  429.4 1.7 reshape.764
  432.2 11.8 all-to-all-start.1
  444.5 2.7 collective-permute-start.2
  447.3 1.9 collective-permute-start.3
  449.2 7.0 all-to-all-done.1
  462.8 4.8 gather_fusion.8
  467.6 2.0 copy.287
  470.9 4.0 scatter_custom_fusion.2
  474.8 190.3 %all-reduce.5 = bf16[16,12288]{0,1:T(8,128)(2,1)} all-reduce(f32[16,12288]{0,1:T(8,128)} %scatter_custom_fusion.2), channel_id=1, replica_groups=mesh['grp'=32,'sub'=16] {'grp','sub'}, use_global_device_ids=true, to_apply=%region_6.11 | all-reduce | flops 196608 | bytes 1179648 | tf_op jit(solution)/shard_map/psum | solution.py:92
  665.1 3.0 fusion.52
  668.1 120.7 %all-gather.1 = bf16[512,24,16]{1,2,0:T(8,128)(2,1)} all-gather(bf16[1,24,16]{1,2,0:T(8,128)(2,1)S(1)} %fusion.52), channel_id=1, replica_groups=mesh['grp'=32,'sub'=16] {'grp','sub'}, dimensions={0}, use_global_device_ids=true | all-gather | bytes 393984 | tf_op jit(solution)/shard_map/all_gather | solution.py:99
  788.8 4.5 copy.331
  793.3 3.0 gather_fusion.9
  798.3 2.8 gather_fusion.11
  801.1 5.1 gather_fusion.10
  808.7 1.7 reshape.766
  811.4 6.2 all-to-all-start.2
  819.0 8.2 collective-permute-start.4
  827.2 3.7 collective-permute-start.5
  837.6 5.1 gather_fusion.12
  845.1 107.2 %all-reduce = (f32[16]{0:T(128)S(1)}, f32[16]{0:T(128)S(1)}) all-reduce(f32[16]{0:T(128)S(1)} %get-tuple-element.15, f32[16]{0:T(128)S(1)} %get-tuple-element.14), channel_id=1, replica_groups=mesh['grp'=32,'sub'=16] {'grp','sub'}, use_global_device_ids=true, to_apply=%region_4.9 | all-reduce | flops 32 | bytes 256 | tf_op jit(solution)/shard_map/psum | solution.py:131
  954.8 1.6 gather_fusion.14
  956.4 2.8 gather_fusion.13
  961.3 8.2 all-to-all-start.3
  970.2 2.8 collective-permute-start.6
  973.0 1.9 collective-permute-start.7
  974.9 6.2 all-to-all-done.3
  982.4 3.7 gather_fusion.15
  987.6 101.6 %psum.53 = f32[16]{0:T(128)S(1)} all-reduce(f32[16]{0:T(128)S(1)} %multiply_reduce_fusion.1), channel_id=1, replica_groups=mesh['grp'=32,'sub'=16] {'grp','sub'}, use_global_device_ids=true, to_apply=%region_10.15 | all-reduce | flops 16 | bytes 128 | tf_op jit(solution)/shard_map/psum | solution.py:131
  1090.3 4.0 scatter_custom_fusion.3
  1094.2 185.3 %all-reduce.6 = bf16[16,12288]{0,1:T(8,128)(2,1)} all-reduce(f32[16,12288]{0,1:T(8,128)} %scatter_custom_fusion.3), channel_id=1, replica_groups=mesh['grp'=32,'sub'=16] {'grp','sub'}, use_global_device_ids=true, to_apply=%region_12.17 | all-reduce | flops 196608 | bytes 1179648 | tf_op jit(solution)/shard_map/psum | solution.py:92
  1279.5 2.8 fusion.55
  1282.3 120.6 %all-gather.2 = bf16[512,24,16]{1,2,0:T(8,128)(2,1)} all-gather(bf16[1,24,16]{1,2,0:T(8,128)(2,1)S(1)} %fusion.55), channel_id=1, replica_groups=mesh['grp'=32,'sub'=16] {'grp','sub'}, dimensions={0}, use_global_device_ids=true | all-gather | bytes 393984 | tf_op jit(solution)/shard_map/all_gather | solution.py:99
  1403.0 4.5 copy.332
  1407.5 3.0 gather_fusion.16
  1411.6 1.6 gather_fusion.18
  1413.2 2.8 gather_fusion.17
  1418.1 8.8 all-to-all-start.4
  1426.9 8.2 collective-permute-start.8
  1435.1 3.1 collective-permute-start.9
  1440.8 2.6 gather_fusion.19
  1444.6 107.4 %psum.55 = f32[16]{0:T(128)S(1)} all-reduce(f32[16]{0:T(128)S(1)} %multiply_reduce_fusion), channel_id=1, replica_groups=mesh['grp'=32,'sub'=16] {'grp','sub'}, use_global_device_ids=true, to_apply=%region_14.19 | all-reduce | flops 16 | bytes 128 | tf_op jit(solution)/shard_map/psum | solution.py:138
  1552.0 1.7 subtract_bitcast_fusion
  (234 shorter events, 71.2 us)
Async XLA Ops:
  0.6 370.3 %copy-start = (bf16[1,1,3,512,512]{4,3,2,1,0:T(8,128)(2,1)S(1)}, bf16[1,1,3,512,512]{4,3,2,1,0:T(8,128)(2,1)}, u32[]{:S(2)}) copy-start(bf16[1,1,3,512,512]{4,3,2,1,0:T(8,128)(2,1)} %param.23) | copy-start | bytes 4718596
  5.5 423.2 %copy-start.15 = (pred[16,64]{1,0:T(8,128)(4,1)}, pred[16,64]{1,0:T(8,128)(4,1)S(1)}, u32[]{:S(2)}) copy-start(pred[16,64]{1,0:T(8,128)(4,1)S(1)} %compare_and_fusion.1) | copy-start | bytes 3076
  7.5 793.5 %copy-start.7 = (s32[1024]{0:T(1024)}, s32[1024]{0:T(1024)S(1)}, u32[]{:S(2)}) copy-start(s32[1024]{0:T(1024)S(1)} %broadcast_clamp_fusion) | copy-start | bytes 12292
  13.7 21.8 %copy-start.17 = (s32[1536]{0:T(1024)}, s32[1536]{0:T(1024)S(1)}, u32[]{:S(2)}) copy-start(s32[1536]{0:T(1024)S(1)} %scatter_custom_fusion) | copy-start | bytes 18436
  13.7 449.1 %copy-start.9 = (s32[2048]{0:T(1024)}, s32[2048]{0:T(1024)S(1)}, u32[]{:S(2)}) copy-start(s32[2048]{0:T(1024)S(1)} %pad_clamp_fusion) | copy-start | bytes 24580
  27.1 8.5 copy-start.22
  27.1 11.8 copy-start.29
  27.1 13.0 copy-start.5
  44.5 195.8 %copy-start.3 = (bf16[24,12288]{1,0:T(8,128)(2,1)S(1)}, bf16[24,12288]{1,0:T(8,128)(2,1)}, u32[]{:S(2)}) copy-start(bf16[24,12288]{1,0:T(8,128)(2,1)} %param.27) | copy-start | bytes 1769476
  363.1 7.5 copy-start.26
  371.7 0.9 copy-start.2
  376.6 41.3 %copy-start.1 = (bf16[1,1,3,512,512]{4,3,2,1,0:T(8,128)(2,1)S(1)}, bf16[1,1,3,512,512]{4,3,2,1,0:T(8,128)(2,1)}, u32[]{:S(2)}) copy-start(bf16[1,1,3,512,512]{4,3,2,1,0:T(8,128)(2,1)} %param.24) | copy-start | bytes 4718596
  380.3 23.6 %all-to-all-start = ((f32[16,1,1024]{2,1,0:T(1,128)}), f32[16,1,1024]{2,1,0:T(1,128)S(1)}, u32[]{:S(2)}, u32[]{:S(2)}) async-start(f32[16,1,1024]{2,1,0:T(1,128)} %reshape.762), calls=%async_computation | async-start | bytes 131072 | tf_op jit(solution)/shard_map/all_to_all | solution.py:71
  387.2 28.7 %copy-start.23 = (pred[2,256]{1,0:T(4,128)(4,1)}, pred[2,256]{1,0:T(4,128)(4,1)S(1)}, u32[]{:S(2)}) copy-start(pred[2,256]{1,0:T(4,128)(4,1)S(1)} %compare_and_fusion.2) | copy-start | bytes 1540
  387.3 2.8 copy-start.18
  391.8 17.4 %collective-permute-start = (f32[16,1,256]{2,0,1:T(8,128)}, f32[16,1,256]{2,0,1:T(8,128)S(1)}, u32[]{:S(2)}, u32[]{:S(2)}) collective-permute-start(f32[16,1,256]{2,0,1:T(8,128)} %get-tuple-element.34), channel_id=1, source_target_pairs={{0,16},{16,32},{32,48},{48,64},{64,80},{80,96},{96,112},{112,128},... | collective-permute-start | bytes 49160 | tf_op jit(solution)/shard_map/ppermute | solution.py:22
  400.0 9.2 collective-permute-start.1
  403.9 65.7 %copy-start.11 = (pred[1536]{0:T(1024)(128)(4,1)}, pred[1536]{0:T(1024)(128)(4,1)S(1)}, u32[]{:S(2)}) copy-start(pred[1536]{0:T(1024)(128)(4,1)S(1)} %compare_and_fusion) | copy-start | bytes 4612
  407.5 12.2 copy-start.19
  418.5 13.7 copy-start.24
  432.2 24.0 %all-to-all-start.1 = ((f32[16,1,1024]{2,1,0:T(1,128)}), f32[16,1,1024]{2,1,0:T(1,128)S(1)}, u32[]{:S(2)}, u32[]{:S(2)}) async-start(f32[16,1,1024]{2,1,0:T(1,128)} %reshape.764), calls=%async_computation.1 | async-start | bytes 131072 | tf_op jit(solution)/shard_map/all_to_all | solution.py:71
  444.5 16.3 %collective-permute-start.2 = (f32[16,1,256]{2,0,1:T(8,128)}, f32[16,1,256]{2,0,1:T(8,128)S(1)}, u32[]{:S(2)}, u32[]{:S(2)}) collective-permute-start(f32[16,1,256]{2,0,1:T(8,128)} %get-tuple-element.32), channel_id=1, source_target_pairs={{0,16},{16,32},{32,48},{48,64},{64,80},{80,96},{96,112},{112,128},... | collective-permute-start | bytes 49160 | tf_op jit(solution)/shard_map/ppermute | solution.py:22
  447.3 13.5 collective-permute-start.3
  449.2 25.7 %copy-start.13 = (f32[1536]{0:T(1024)}, f32[1536]{0:T(1024)S(1)}, u32[]{:S(2)}) copy-start(f32[1536]{0:T(1024)S(1)} %broadcast_multiply_fusion) | copy-start | bytes 18436
  788.8 7.5 copy-start.27
  788.8 9.5 copy-start.20
  811.4 19.4 %all-to-all-start.2 = ((f32[16,1,1024]{2,1,0:T(1,128)}), f32[16,1,1024]{2,1,0:T(1,128)S(1)}, u32[]{:S(2)}, u32[]{:S(2)}) async-start(f32[16,1,1024]{2,1,0:T(1,128)} %reshape.766), calls=%async_computation.2 | async-start | bytes 131072 | tf_op jit(solution)/shard_map/all_to_all | solution.py:71
  819.0 16.5 %collective-permute-start.4 = (f32[16,1,256]{2,0,1:T(8,128)}, f32[16,1,256]{2,0,1:T(8,128)}, u32[]{:S(2)}, u32[]{:S(2)}) collective-permute-start(f32[16,1,256]{2,0,1:T(8,128)} %get-tuple-element.30), channel_id=1, source_target_pairs={{0,16},{16,32},{32,48},{48,64},{64,80},{80,96},{96,112},{112,128},... | collective-permute-start | bytes 49160 | tf_op jit(solution)/shard_map/ppermute | solution.py:22
  827.2 8.3 collective-permute-start.5
  833.9 118.4 %copy-start.12 = (pred[1536]{0:T(1024)(128)(4,1)S(1)}, pred[1536]{0:T(1024)(128)(4,1)}, u32[]{:S(2)}) copy-start(pred[1536]{0:T(1024)(128)(4,1)} %copy-done.11) | copy-start | bytes 4612
  836.4 118.4 %copy-start.21 = (s32[1024]{0:T(1024)S(1)}, s32[1024]{0:T(1024)}, u32[]{:S(2)}) copy-start(s32[1024]{0:T(1024)} %copy-done.18) | copy-start | bytes 12292
  836.4 120.0 %copy-start.8 = (s32[1024]{0:T(1024)S(1)}, s32[1024]{0:T(1024)}, u32[]{:S(2)}) copy-start(s32[1024]{0:T(1024)} %copy-done.7) | copy-start | bytes 12292
  842.7 116.8 %copy-start.16 = (pred[16,64]{1,0:T(8,128)(4,1)S(1)}, pred[16,64]{1,0:T(8,128)(4,1)}, u32[]{:S(2)}) copy-start(pred[16,64]{1,0:T(8,128)(4,1)} %copy-done.15) | copy-start | bytes 3076
  952.3 2.4 copy-start.34
  952.3 1.6 copy-start.30
  954.5 28.0 %copy-start.10 = (s32[2048]{0:T(1024)S(1)}, s32[2048]{0:T(1024)}, u32[]{:S(2)}) copy-start(s32[2048]{0:T(1024)} %copy-done.9) | copy-start | bytes 24580
  956.4 31.0 %copy-start.6 = (f32[16,1536]{1,0:T(8,128)S(1)}, f32[16,1536]{1,0:T(8,128)}, u32[]{:S(2)}) copy-start(f32[16,1536]{1,0:T(8,128)} %get-tuple-element.21) | copy-start | bytes 294916
  956.4 31.0 %copy-start.14 = (f32[1536]{0:T(1024)S(1)}, f32[1536]{0:T(1024)}, u32[]{:S(2)}) copy-start(f32[1536]{0:T(1024)} %copy-done.13) | copy-start | bytes 18436
  956.4 132.8 %copy-start.35 = (f32[16]{0:T(128)S(1)}, f32[16]{0:T(128)}, u32[]{:S(2)}) copy-start(f32[16]{0:T(128)} %copy-done.34) | copy-start | bytes 196
  961.3 19.8 %all-to-all-start.3 = ((f32[16,1,1024]{2,1,0:T(1,128)}), f32[16,1,1024]{2,1,0:T(1,128)S(1)}, u32[]{:S(2)}, u32[]{:S(2)}) async-start(f32[16,1,1024]{2,1,0:T(1,128)} %reshape.768), calls=%async_computation.3 | async-start | bytes 131072 | tf_op jit(solution)/shard_map/all_to_all | solution.py:71
  970.2 11.9 collective-permute-start.6
  973.0 9.1 collective-permute-start.7
  1089.2 5.0 copy-start.32
  1094.2 185.3 %copy-start.4 = (bf16[24,12288]{1,0:T(8,128)(2,1)S(1)}, bf16[24,12288]{1,0:T(8,128)(2,1)}, u32[]{:S(2)}) copy-start(bf16[24,12288]{1,0:T(8,128)(2,1)} %param.27) | copy-start | bytes 1769476
  1403.0 7.5 copy-start.28
  1407.5 19.4 %copy-start.25 = (pred[2,256]{1,0:T(4,128)(4,1)S(1)}, pred[2,256]{1,0:T(4,128)(4,1)}, u32[]{:S(2)}) copy-start(pred[2,256]{1,0:T(4,128)(4,1)} %copy-done.23) | copy-start | bytes 1540
  1413.2 138.8 %copy-start.33 = (f32[16]{0:T(128)S(1)}, f32[16]{0:T(128)}, u32[]{:S(2)}) copy-start(f32[16]{0:T(128)} %copy-done.32) | copy-start | bytes 196
  1413.2 138.8 %copy-start.31 = (f32[16]{0:T(128)S(1)}, f32[16]{0:T(128)}, u32[]{:S(2)}) copy-start(f32[16]{0:T(128)} %copy-done.30) | copy-start | bytes 196
  1418.1 20.4 %all-to-all-start.4 = ((f32[16,1,1024]{2,1,0:T(1,128)}), f32[16,1,1024]{2,1,0:T(1,128)S(1)}, u32[]{:S(2)}, u32[]{:S(2)}) async-start(f32[16,1,1024]{2,1,0:T(1,128)} %reshape.770), calls=%async_computation.4 | async-start | bytes 131072 | tf_op jit(solution)/shard_map/all_to_all | solution.py:71
  1426.9 12.6 collective-permute-start.8
  1435.1 5.4 collective-permute-start.9
where the time goes:
time: 1560 us; the launch traced here: 1550 us
  blocking collectives  1250 us (80%)
  local copies, waits for them, and re-layouts  140 us (9%)
  starting transfers between devices  85.2 us (5%)
  other arithmetic  50.4 us (3%)
    psum x3, blocking collectives, apply_tilde(): coarse_load = lax.psum(partial_load, ('grp', 'sub'))  571 us
    all_gather x3, blocking collectives, apply_tilde(): lax.all_gather(owned_values, ('grp', 'sub'), axis=1, tiled=True)  361 us
    psum x2, blocking collectives, per_device(): inner_now = lax.psum(jnp.sum(residual * precond, axis=1), ('grp', 'sub'))  209 us
    psum x1, blocking collectives, per_device(): curvature = lax.psum(jnp.sum(search * image, axis=1), ('grp', 'sub'))  107 us
    all_to_all x5, starting transfers between devices, partner(): lax.all_to_all(outgoing, 'sub', split_axis=1, concat_axis=1, tiled=True)  41.3 us
  transfers between devices with their start and end apart: 15, of which 4 were waited for; matrix products, arithmetic and copies ran while one was open for 2% of the time, Pallas kernels for 0%

commit v1 on v0

--- a/solution.py
+++ b/solution.py
@@ -96,7 +96,12 @@
             coarse_inverse,
             preferred_element_type=jnp.float32,
         )
-        coarse_values = lax.all_gather(owned_values, ("grp", "sub"), axis=1, tiled=True)
+        coarse_values = jnp.concatenate(
+            lax.all_to_all(
+                jnp.stack([owned_values] * lax.axis_size(("grp", "sub"))), ("grp", "sub"), 0, 0
+            ),
+            axis=1,
+        )
         at_corners = (
             jnp.take(coarse_values, corner_index, axis=1)
             .astype(jnp.bfloat16)

time: 1560 us -> 1340 us (0.86)
  blocking collectives: 1250 us -> 972 us
  waiting for transfers between devices: 14.4 us -> 64.4 us
  local copies, waits for them, and re-layouts: 140 us -> 163 us
  starting transfers between devices: 85.2 us -> 63.7 us
    all_gather x3 -> x0, blocking collectives: 361 us -> none  [apply_tilde(): lax.all_gather(owned_values, ('grp', 'sub'), axis=1, tiled=True)]
    all_to_all x0 -> x2, blocking collectives: none -> 102 us  [apply_tilde(): lax.all_to_all(jnp.stack([owned_values] * lax.axis_size(('grp', 'sub'))),...]
    all_to_all x0 -> x1, waiting for transfers between devices: none -> 34.4 us  [apply_tilde(): lax.all_to_all(jnp.stack([owned_values] * lax.axis_size(('grp', 'sub'))),...]
    all_to_all x5, waiting for transfers between devices: 13.4 us -> 30 us  [partner(): lax.all_to_all(outgoing, 'sub', split_axis=1, concat_axis=1, tiled=True)]
    ppermute x5, starting transfers between devices: 30.1 us -> 14 us  [extended(): lax.ppermute(tail, axis, [(i, (i + 1) % count) for i in range(ends)])]
    all_to_all x5, starting transfers between devices: 41.3 us -> 25.4 us  [partner(): lax.all_to_all(outgoing, 'sub', split_axis=1, concat_axis=1, tiled=True)]
    unnamed x87 -> x86, local copies, waits for them, and re-layouts: 25.7 us -> 33.2 us
  transfers between devices with their start and end apart: 15 -> 16, of which waited for: 4 -> 6; matrix products, arithmetic and copies ran while one was open for 2% -> 2% of each run, Pallas kernels for 0% -> 0%
where the time goes in v1:
time: 1340 us; the launch traced here: 1330 us
  blocking collectives  972 us (73%)
  local copies, waits for them, and re-layouts  163 us (12%)
  waiting for transfers between devices  64.4 us (5%)
  starting transfers between devices  63.7 us (5%)
  other arithmetic  50.6 us (4%)
  matrix products  13.4 us (1%)
    psum x3, blocking collectives, apply_tilde(): coarse_load = lax.psum(partial_load, ('grp', 'sub'))  569 us
    psum x2, blocking collectives, per_device(): inner_now = lax.psum(jnp.sum(residual * precond, axis=1), ('grp', 'sub'))  201 us
    all_to_all x2, blocking collectives, apply_tilde(): lax.all_to_all(jnp.stack([owned_values] * lax.axis_size(('grp', 'sub'))),...  102 us
    psum x1, blocking collectives, per_device(): curvature = lax.psum(jnp.sum(search * image, axis=1), ('grp', 'sub'))  100 us
    all_to_all x1, waiting for transfers between devices, apply_tilde(): lax.all_to_all(jnp.stack([owned_values] * lax.axis_size(('grp', 'sub'))),...  34.4 us
    unnamed x86, local copies, waits for them, and re-layouts  33.2 us
    all_to_all x5, waiting for transfers between devices, partner(): lax.all_to_all(outgoing, 'sub', split_axis=1, concat_axis=1, tiled=True)  30 us
    gather x10, local copies, waits for them, and re-layouts, partner(): return jnp.take(joined, slot_inverse, axis=1)  27.3 us
  transfers between devices with their start and end apart: 16, of which 6 were waited for; matrix products, arithmetic and copies ran while one was open for 2% of the time, Pallas kernels for 0%

profile of v1, /device:TPU:1, one launch (start us, length us, event | category | flops | bytes accessed | tf_op | source)
XLA Modules:
  0.0 1329.5 jit_solution(8438843050691314655)
XLA Ops:
  4.8 6.2 scatter_custom_fusion
  11.1 2.0 fusion.112
  13.1 4.5 fusion.93
  17.6 6.9 fusion.91
  24.5 8.4 gather_fusion
  37.8 4.0 scatter_custom_fusion.1
  41.8 195.8 %all-reduce.4 = bf16[16,12288]{0,1:T(8,128)(2,1)} all-reduce(f32[16,12288]{0,1:T(8,128)} %scatter_custom_fusion.1), channel_id=1, replica_groups=mesh['grp'=32,'sub'=16] {'grp','sub'}, use_global_device_ids=true, to_apply=%region_2.3 | all-reduce | flops 196608 | bytes 1179648 | tf_op jit(solution)/shard_map/psum | solution.py:92
  237.6 2.8 fusion.120
  242.1 4.4 reshape.786
  246.5 14.1 %all-to-all-start = ((bf16[512,2,192]{2,1,0:T(2,128)(2,1)}), bf16[512,2,192]{2,1,0:T(2,128)(2,1)S(1)}, u32[]{:S(2)}, u32[]{:S(2)}) async-start(bf16[512,2,192]{2,1,0:T(2,128)(2,1)} %reshape.786), calls=%async_computation | async-start | bytes 1048576 | tf_op jit(solution)/shard_map/all_to_all | solution.py:100
  261.6 34.4 %all-to-all-done = bf16[512,2,192]{2,1,0:T(2,128)(2,1)S(1)} async-done(((bf16[512,2,192]{2,1,0:T(2,128)(2,1)}), bf16[512,2,192]{2,1,0:T(2,128)(2,1)S(1)}, u32[]{:S(2)}, u32[]{:S(2)}) %all-to-all-start) | async-done | bytes 393248 | tf_op jit(solution)/shard_map/all_to_all | solution.py:100
  296.0 2.7 reshape.787
  298.6 4.5 copy.259
  303.1 2.9 gather_fusion.2
  308.8 4.0 gather_fusion.3
  317.5 3.5 all-to-all-start.1
  322.3 2.5 collective-permute-start
  324.8 1.9 collective-permute-start.1
  327.5 5.2 all-to-all-done.1
  339.8 4.8 gather_fusion.5
  348.3 2.8 gather_fusion.7
  351.1 5.1 gather_fusion.6
  361.5 6.6 all-to-all-start.2
  368.7 3.9 collective-permute-start.2
  374.5 5.9 all-to-all-done.2
  387.1 4.8 gather_fusion.8
  391.9 2.0 copy.277
  395.2 4.0 scatter_custom_fusion.2
  399.2 188.0 %all-reduce.5 = bf16[16,12288]{0,1:T(8,128)(2,1)} all-reduce(f32[16,12288]{0,1:T(8,128)} %scatter_custom_fusion.2), channel_id=1, replica_groups=mesh['grp'=32,'sub'=16] {'grp','sub'}, use_global_device_ids=true, to_apply=%region_6.11 | all-reduce | flops 196608 | bytes 1179648 | tf_op jit(solution)/shard_map/psum | solution.py:92
  587.2 3.0 fusion.119
  591.8 4.4 reshape.792
  596.1 49.9 %all_to_all.40 = bf16[512,2,192]{2,1,0:T(2,128)(2,1)} all-to-all(bf16[512,2,192]{2,1,0:T(2,128)(2,1)} %reshape.792), channel_id=1, replica_groups=mesh['grp'=32,'sub'=16] {'grp','sub'}, dimensions={0} | all-to-all | bytes 786432 | tf_op jit(solution)/shard_map/all_to_all | solution.py:100
  646.0 4.2 reshape.793
  650.2 4.5 copy.282
  654.7 3.0 gather_fusion.9
  659.7 2.8 gather_fusion.11
  662.5 5.1 gather_fusion.10
  672.9 3.5 all-to-all-start.4
  677.7 2.4 collective-permute-start.4
  680.1 2.5 collective-permute-start.5
  682.6 5.4 all-to-all-done.4
  694.7 5.1 gather_fusion.12
  702.3 99.4 %all-reduce = (f32[16]{0:T(128)S(1)}, f32[16]{0:T(128)S(1)}) all-reduce(f32[16]{0:T(128)S(1)} %get-tuple-element.15, f32[16]{0:T(128)S(1)} %get-tuple-element.14), channel_id=1, replica_groups=mesh['grp'=32,'sub'=16] {'grp','sub'}, use_global_device_ids=true, to_apply=%region_4.9 | all-reduce | flops 32 | bytes 256 | tf_op jit(solution)/shard_map/psum | solution.py:136
  805.8 2.8 gather_fusion.13
  810.6 8.2 all-to-all-start.5
  819.5 2.7 collective-permute-start.6
  822.2 1.9 collective-permute-start.7
  824.1 6.3 all-to-all-done.5
  831.8 3.7 gather_fusion.15
  836.9 101.9 %psum.53 = f32[16]{0:T(128)S(1)} all-reduce(f32[16]{0:T(128)S(1)} %multiply_reduce_fusion.1), channel_id=1, replica_groups=mesh['grp'=32,'sub'=16] {'grp','sub'}, use_global_device_ids=true, to_apply=%region_10.15 | all-reduce | flops 16 | bytes 128 | tf_op jit(solution)/shard_map/psum | solution.py:136
  939.9 4.0 scatter_custom_fusion.3
  943.8 185.1 %all-reduce.6 = bf16[16,12288]{0,1:T(8,128)(2,1)} all-reduce(f32[16,12288]{0,1:T(8,128)} %scatter_custom_fusion.3), channel_id=1, replica_groups=mesh['grp'=32,'sub'=16] {'grp','sub'}, use_global_device_ids=true, to_apply=%region_12.17 | all-reduce | flops 196608 | bytes 1179648 | tf_op jit(solution)/shard_map/psum | solution.py:92
  1129.0 2.8 fusion.118
  1133.4 3.7 reshape.798
  1137.1 52.0 %all_to_all.41 = bf16[512,2,192]{2,1,0:T(2,128)(2,1)S(1)} all-to-all(bf16[512,2,192]{2,1,0:T(2,128)(2,1)S(1)} %reshape.798), channel_id=1, replica_groups=mesh['grp'=32,'sub'=16] {'grp','sub'}, dimensions={0} | all-to-all | bytes 786432 | tf_op jit(solution)/shard_map/all_to_all | solution.py:100
  1189.1 2.7 reshape.799
  1191.7 4.5 copy.305
  1196.2 3.0 gather_fusion.16
  1202.0 2.8 gather_fusion.17
  1206.8 3.5 all-to-all-start.7
  1210.4 2.5 collective-permute-start.8
  1214.8 7.2 all-to-all-done.7
  1223.3 2.6 gather_fusion.19
  1227.2 100.5 %psum.55 = f32[16]{0:T(128)S(1)} all-reduce(f32[16]{0:T(128)S(1)} %multiply_reduce_fusion), channel_id=1, replica_groups=mesh['grp'=32,'sub'=16] {'grp','sub'}, use_global_device_ids=true, to_apply=%region_14.19 | all-reduce | flops 16 | bytes 128 | tf_op jit(solution)/shard_map/psum | solution.py:143
  (240 shorter events, 90.0 us)
Async XLA Ops:
  0.6 305.7 %copy-start = (bf16[1,1,3,512,512]{4,3,2,1,0:T(8,128)(2,1)S(1)}, bf16[1,1,3,512,512]{4,3,2,1,0:T(8,128)(2,1)}, u32[]{:S(2)}) copy-start(bf16[1,1,3,512,512]{4,3,2,1,0:T(8,128)(2,1)} %param.23) | copy-start | bytes 4718596
  11.0 6.6 copy-start.16
  11.1 376.0 %copy-start.8 = (s32[2048]{0:T(1024)}, s32[2048]{0:T(1024)S(1)}, u32[]{:S(2)}) copy-start(s32[2048]{0:T(1024)S(1)} %pad_clamp_fusion) | copy-start | bytes 24580
  24.5 8.4 copy-start.21
  24.5 13.0 copy-start.4
  41.8 195.8 %copy-start.2 = (bf16[24,12288]{1,0:T(8,128)(2,1)S(1)}, bf16[24,12288]{1,0:T(8,128)(2,1)}, u32[]{:S(2)}) copy-start(bf16[24,12288]{1,0:T(8,128)(2,1)} %param.27) | copy-start | bytes 1769476
  240.5 20.1 %copy-start.23 = (s32[1,1,1536]{2,1,0:T(1,128)S(1)}, s32[1,1,1536]{2,1,0:T(1,128)}, u32[]{:S(2)}) copy-start(s32[1,1,1536]{2,1,0:T(1,128)} %param.29) | copy-start | bytes 18436
  246.5 49.5 %all-to-all-start = ((bf16[512,2,192]{2,1,0:T(2,128)(2,1)}), bf16[512,2,192]{2,1,0:T(2,128)(2,1)S(1)}, u32[]{:S(2)}, u32[]{:S(2)}) async-start(bf16[512,2,192]{2,1,0:T(2,128)(2,1)} %reshape.786), calls=%async_computation | async-start | bytes 1048576 | tf_op jit(solution)/shard_map/all_to_all | solution.py:100
  260.9 46.2 %copy-start.17 = (s32[1024]{0:T(1024)}, s32[1024]{0:T(1024)S(1)}, u32[]{:S(2)}) copy-start(s32[1024]{0:T(1024)S(1)} %pad_clamp_fusion.1) | copy-start | bytes 12292
  261.0 42.2 %copy-start.24 = (s32[1024]{0:T(1024)}, s32[1024]{0:T(1024)S(1)}, u32[]{:S(2)}) copy-start(s32[1024]{0:T(1024)S(1)} %pad_clamp_fusion.2) | copy-start | bytes 12292
  261.0 45.1 %copy-start.25 = (pred[72]{0:T(512)(128)(4,1)}, pred[72]{0:T(512)(128)(4,1)S(1)}, u32[]{:S(2)}) copy-start(pred[72]{0:T(512)(128)(4,1)S(1)} %compare_and_fusion.3) | copy-start | bytes 220
  261.6 400.9 %copy-start.6 = (s32[1024]{0:T(1024)}, s32[1024]{0:T(1024)S(1)}, u32[]{:S(2)}) copy-start(s32[1024]{0:T(1024)S(1)} %broadcast_clamp_fusion) | copy-start | bytes 12292
  261.6 95.8 %copy-start.14 = (pred[16,64]{1,0:T(8,128)(4,1)}, pred[16,64]{1,0:T(8,128)(4,1)S(1)}, u32[]{:S(2)}) copy-start(pred[16,64]{1,0:T(8,128)(4,1)S(1)} %compare_and_fusion.1) | copy-start | bytes 3076
  312.8 33.9 %copy-start.1 = (bf16[1,1,3,512,512]{4,3,2,1,0:T(8,128)(2,1)S(1)}, bf16[1,1,3,512,512]{4,3,2,1,0:T(8,128)(2,1)}, u32[]{:S(2)}) copy-start(bf16[1,1,3,512,512]{4,3,2,1,0:T(8,128)(2,1)} %param.24) | copy-start | bytes 4718596
  317.5 15.2 %all-to-all-start.1 = ((f32[16,1,1024]{2,1,0:T(1,128)}), f32[16,1,1024]{2,1,0:T(1,128)S(1)}, u32[]{:S(2)}, u32[]{:S(2)}) async-start(f32[16,1,1024]{2,1,0:T(1,128)} %reshape.788), calls=%async_computation.1 | async-start | bytes 131072 | tf_op jit(solution)/shard_map/all_to_all | solution.py:71
  322.3 15.5 %collective-permute-start = (f32[16,1,256]{2,0,1:T(8,128)}, f32[16,1,256]{2,0,1:T(8,128)S(1)}, u32[]{:S(2)}, u32[]{:S(2)}) collective-permute-start(f32[16,1,256]{2,0,1:T(8,128)} %get-tuple-element.34), channel_id=1, source_target_pairs={{0,16},{16,32},{32,48},{48,64},{64,80},{80,96},{96,112},{112,128},... | collective-permute-start | bytes 49160 | tf_op jit(solution)/shard_map/ppermute | solution.py:22
  324.8 13.0 collective-permute-start.1
  327.5 66.5 %copy-start.10 = (pred[1536]{0:T(1024)(128)(4,1)}, pred[1536]{0:T(1024)(128)(4,1)S(1)}, u32[]{:S(2)}) copy-start(pred[1536]{0:T(1024)(128)(4,1)S(1)} %compare_and_fusion) | copy-start | bytes 4612
  336.2 12.2 copy-start.18
  361.5 19.0 %all-to-all-start.2 = ((f32[16,1,1024]{2,1,0:T(1,128)}), f32[16,1,1024]{2,1,0:T(1,128)S(1)}, u32[]{:S(2)}, u32[]{:S(2)}) async-start(f32[16,1,1024]{2,1,0:T(1,128)} %reshape.790), calls=%async_computation.2 | async-start | bytes 131072 | tf_op jit(solution)/shard_map/all_to_all | solution.py:71
  368.7 16.4 %collective-permute-start.2 = (f32[16,1,256]{2,0,1:T(8,128)}, f32[16,1,256]{2,0,1:T(8,128)S(1)}, u32[]{:S(2)}, u32[]{:S(2)}) collective-permute-start(f32[16,1,256]{2,0,1:T(8,128)} %get-tuple-element.32), channel_id=1, source_target_pairs={{0,16},{16,32},{32,48},{48,64},{64,80},{80,96},{96,112},{112,128},... | collective-permute-start | bytes 49160 | tf_op jit(solution)/shard_map/ppermute | solution.py:22
  372.6 12.5 collective-permute-start.3
  374.5 24.6 %copy-start.12 = (f32[1536]{0:T(1024)}, f32[1536]{0:T(1024)S(1)}, u32[]{:S(2)}) copy-start(f32[1536]{0:T(1024)S(1)} %broadcast_multiply_fusion) | copy-start | bytes 18436
  650.2 7.5 copy-start.26
  650.2 9.5 copy-start.19
  672.9 15.2 %all-to-all-start.4 = ((f32[16,1,1024]{2,1,0:T(1,128)}), f32[16,1,1024]{2,1,0:T(1,128)S(1)}, u32[]{:S(2)}, u32[]{:S(2)}) async-start(f32[16,1,1024]{2,1,0:T(1,128)} %reshape.794), calls=%async_computation.4 | async-start | bytes 131072 | tf_op jit(solution)/shard_map/all_to_all | solution.py:71
  677.7 15.0 %collective-permute-start.4 = (f32[16,1,256]{2,0,1:T(8,128)}, f32[16,1,256]{2,0,1:T(8,128)}, u32[]{:S(2)}, u32[]{:S(2)}) collective-permute-start(f32[16,1,256]{2,0,1:T(8,128)} %get-tuple-element.30), channel_id=1, source_target_pairs={{0,16},{16,32},{32,48},{48,64},{64,80},{80,96},{96,112},{112,128},... | collective-permute-start | bytes 49160 | tf_op jit(solution)/shard_map/ppermute | solution.py:22
  680.1 12.6 collective-permute-start.5
  691.0 110.6 %copy-start.11 = (pred[1536]{0:T(1024)(128)(4,1)S(1)}, pred[1536]{0:T(1024)(128)(4,1)}, u32[]{:S(2)}) copy-start(pred[1536]{0:T(1024)(128)(4,1)} %copy-done.10) | copy-start | bytes 4612
  693.5 110.5 %copy-start.20 = (s32[1024]{0:T(1024)S(1)}, s32[1024]{0:T(1024)}, u32[]{:S(2)}) copy-start(s32[1024]{0:T(1024)} %copy-done.17) | copy-start | bytes 12292
  693.6 112.2 %copy-start.7 = (s32[1024]{0:T(1024)S(1)}, s32[1024]{0:T(1024)}, u32[]{:S(2)}) copy-start(s32[1024]{0:T(1024)} %copy-done.6) | copy-start | bytes 12292
  699.8 108.9 %copy-start.15 = (pred[16,64]{1,0:T(8,128)(4,1)S(1)}, pred[16,64]{1,0:T(8,128)(4,1)}, u32[]{:S(2)}) copy-start(pred[16,64]{1,0:T(8,128)(4,1)} %copy-done.14) | copy-start | bytes 3076
  801.6 2.4 copy-start.32
  801.6 1.6 copy-start.28
  803.8 28.0 %copy-start.9 = (s32[2048]{0:T(1024)S(1)}, s32[2048]{0:T(1024)}, u32[]{:S(2)}) copy-start(s32[2048]{0:T(1024)} %copy-done.8) | copy-start | bytes 24580
  805.7 31.0 %copy-start.5 = (f32[16,1536]{1,0:T(8,128)S(1)}, f32[16,1536]{1,0:T(8,128)}, u32[]{:S(2)}) copy-start(f32[16,1536]{1,0:T(8,128)} %get-tuple-element.21) | copy-start | bytes 294916
  805.7 31.0 %copy-start.13 = (f32[1536]{0:T(1024)S(1)}, f32[1536]{0:T(1024)}, u32[]{:S(2)}) copy-start(f32[1536]{0:T(1024)} %copy-done.12) | copy-start | bytes 18436
  805.8 133.1 %copy-start.33 = (f32[16]{0:T(128)S(1)}, f32[16]{0:T(128)}, u32[]{:S(2)}) copy-start(f32[16]{0:T(128)} %copy-done.32) | copy-start | bytes 196
  810.6 19.8 %all-to-all-start.5 = ((f32[16,1,1024]{2,1,0:T(1,128)}), f32[16,1,1024]{2,1,0:T(1,128)S(1)}, u32[]{:S(2)}, u32[]{:S(2)}) async-start(f32[16,1,1024]{2,1,0:T(1,128)} %reshape.796), calls=%async_computation.5 | async-start | bytes 131072 | tf_op jit(solution)/shard_map/all_to_all | solution.py:71
  819.5 11.9 collective-permute-start.6
  822.2 9.2 collective-permute-start.7
  938.8 5.0 copy-start.30
  943.8 185.1 %copy-start.3 = (bf16[24,12288]{1,0:T(8,128)(2,1)S(1)}, bf16[24,12288]{1,0:T(8,128)(2,1)}, u32[]{:S(2)}) copy-start(bf16[24,12288]{1,0:T(8,128)(2,1)} %param.27) | copy-start | bytes 1769476
  1191.7 7.5 copy-start.27
  1196.2 14.1 %copy-start.22 = (pred[2,256]{1,0:T(4,128)(4,1)S(1)}, pred[2,256]{1,0:T(4,128)(4,1)}, u32[]{:S(2)}) copy-start(pred[2,256]{1,0:T(4,128)(4,1)} %compare_and_fusion.2) | copy-start | bytes 1540
  1202.0 125.6 %copy-start.31 = (f32[16]{0:T(128)S(1)}, f32[16]{0:T(128)}, u32[]{:S(2)}) copy-start(f32[16]{0:T(128)} %copy-done.30) | copy-start | bytes 196
  1202.0 125.6 %copy-start.29 = (f32[16]{0:T(128)S(1)}, f32[16]{0:T(128)}, u32[]{:S(2)}) copy-start(f32[16]{0:T(128)} %copy-done.28) | copy-start | bytes 196
  1206.8 15.2 %all-to-all-start.7 = ((f32[16,1,1024]{2,1,0:T(1,128)}), f32[16,1,1024]{2,1,0:T(1,128)S(1)}, u32[]{:S(2)}, u32[]{:S(2)}) async-start(f32[16,1,1024]{2,1,0:T(1,128)} %reshape.800), calls=%async_computation.7 | async-start | bytes 131072 | tf_op jit(solution)/shard_map/all_to_all | solution.py:71
  1210.4 12.6 collective-permute-start.8
  1212.9 10.1 collective-permute-start.9
